TPU v7x, 32 devices: a whole 2x2x4 slice. The times are simulated.
32 devices in a mesh: groups: 2 (over x), seq: 16 (over z, y, core).
Axes of the slice: x: 2, y: 2, z: 4, core: 2. Of those that a mesh axis runs over, the one named last changes fastest.
Arguments:
- queries: bfloat16 [16384, 1536], P(('groups', 'seq')), parts along dimension 0, may hold values from -5 to 5
- key_vectors: bfloat16 [16384, 1536], P(('groups', 'seq')), parts along dimension 0, may hold values from -5 to 5
- value_vectors: bfloat16 [16384, 1536], P(('groups', 'seq')), parts along dimension 0, may hold values from -6 to 6
- hidden: bfloat16 [16384, 1536], P(('groups', 'seq')), parts along dimension 0, may hold values from -6 to 6
- out_weight: bfloat16 [1536, 1536], replicated, may hold values from -0.15625 to 0.15625
- conv_weight: bfloat16 [31, 1536], replicated, may hold values from -1 to 1
- cotangent: bfloat16 [16384, 1536], P(('groups', 'seq')), parts along dimension 0, may hold values from -6 to 6
- valid_mask: int32 [16384], P(('groups', 'seq')), parts along dimension 0, may hold values from 0 to 1, as said below
Outputs:
- grad_queries: bfloat16 [16384, 1536], P(('groups', 'seq')), parts along dimension 0
- grad_keys: bfloat16 [16384, 1536], P(('groups', 'seq')), parts along dimension 0
- grad_values: bfloat16 [16384, 1536], P(('groups', 'seq')), parts along dimension 0
- grad_hidden: bfloat16 [16384, 1536], P(('groups', 'seq')), parts along dimension 0
- grad_out_weight: float32 [3072, 1536], P(('groups', 'seq')), parts along dimension 0
- grad_conv_weight: float32 [62, 1536], P('groups'), parts along dimension 0
There are 2 independent parts, one for each index of `groups`. A program takes and returns all parts, laid end to end along the dimension named above; an argument that names none is the same for every part. Nothing has to cross between parts.
Inputs may be any that keep to these rules, and one draw needn't show every extreme that they name: valid_mask is 1 on the frames before a length and 0 from it on; the length lies between 8065 and 8191.
All inputs are finite; a program needn't handle non-finite values.
Results may differ from a plain program's by a relative error of at most 0.019.
Values may be sent and summed in bfloat16 or wider, within the bound.
No kernel may reach another device: no remote copies, remote signals or barrier semaphores. Data moves between devices by JAX's collectives and lax.ppermute only.
A program may use at most 128 MiB of HBM per device.

v0:
```python
import math

import jax
import jax.numpy as jnp
from jax import lax
from jax.sharding import PartitionSpec as P

HEADS = 16
KERNEL = 31
BLOCK = 128


def shifted(value, axis, steps):
    count = lax.axis_size(axis)
    initial, last = (max(0, -steps), min(count, count - steps))
    return lax.ppermute(value, axis, [(source, source + steps) for source in range(initial, last)])


def window_of(extended, block_count, tail_shape):
    frames = extended.shape[0] - BLOCK
    earlier = extended[:frames].reshape((block_count, BLOCK) + tail_shape)
    current = extended[BLOCK:].reshape((block_count, BLOCK) + tail_shape)
    return jnp.concatenate([earlier, current], axis=1)


def per_device(
    queries, key_vectors, value_vectors, hidden, out_weight, conv_weight, cotangent, valid_mask
):
    frames, features = queries.shape
    head_size = features // HEADS
    block_count = frames // BLOCK
    rim_rows = KERNEL - 1
    score_scale = 1.0 / math.sqrt(head_size)
    first_dev = lax.axis_index("seq") == 0
    context_k, context_v = shifted(
        (key_vectors[frames - BLOCK :], value_vectors[frames - BLOCK :]), "seq", 1
    )
    cot_next = shifted(cotangent[:rim_rows], "seq", -1)
    upstream = cotangent.astype(jnp.float32)
    upstream_next = cot_next.astype(jnp.float32)
    conv_taps = conv_weight.astype(jnp.float32)
    padded = jnp.concatenate([upstream, upstream_next], axis=0)
    running = jnp.zeros((frames, features), jnp.float32)
    for offset in range(KERNEL):
        running = running + conv_taps[offset] * padded[offset : offset + frames]
    grad_hidden = running.astype(jnp.bfloat16)
    hidden_vals = hidden.astype(jnp.float32)
    tap_rows = []
    hidden_prev = shifted(hidden[frames - rim_rows :], "seq", 1)
    hidden_pad = jnp.concatenate([hidden_prev.astype(jnp.float32), hidden_vals], axis=0)
    for offset in range(KERNEL):
        tap_rows.append(
            jnp.sum(hidden_pad[rim_rows - offset : rim_rows - offset + frames] * upstream, axis=0)
        )
    grad_conv_weight = lax.psum(jnp.stack(tap_rows, axis=0), "seq")
    grad_attended = lax.dot_general(
        grad_hidden, out_weight, (((1,), (1,)), ((), ())), preferred_element_type=jnp.float32
    ).astype(jnp.bfloat16)
    context_mask = jnp.where(first_dev, 0, 1) * jnp.ones((BLOCK,), jnp.int32)
    key_ext = jnp.concatenate([context_k, key_vectors], axis=0)
    value_ext = jnp.concatenate([context_v, value_vectors], axis=0)
    mask_ext = jnp.concatenate([context_mask, valid_mask], axis=0)
    head_shape = (HEADS, head_size)
    key_windows = window_of(
        key_ext.reshape((frames + BLOCK,) + head_shape), block_count, head_shape
    )
    value_windows = window_of(
        value_ext.reshape((frames + BLOCK,) + head_shape), block_count, head_shape
    )
    mask_windows = window_of(mask_ext, block_count, ())
    query_blocks = queries.reshape(block_count, BLOCK, HEADS, head_size)
    grad_blocks = grad_attended.reshape(block_count, BLOCK, HEADS, head_size)
    scores = (
        jnp.einsum("cqhd,ckhd->chqk", query_blocks, key_windows, preferred_element_type=jnp.float32)
        * score_scale
    )
    allowed = (mask_windows == 1)[:, None, None, :]
    row_max = jnp.max(jnp.where(allowed, scores, -1e30), axis=-1, keepdims=True)
    weights_raw = jnp.where(allowed, jnp.exp(scores - row_max), 0.0)
    probs = weights_raw / jnp.sum(weights_raw, axis=-1, keepdims=True)
    probs_b = probs.astype(jnp.bfloat16)
    attended = jnp.einsum(
        "chqk,ckhd->cqhd", probs_b, value_windows, preferred_element_type=jnp.float32
    ).astype(jnp.bfloat16)
    dprobs = jnp.einsum(
        "cqhd,ckhd->chqk", grad_blocks, value_windows, preferred_element_type=jnp.float32
    )
    delta = jnp.einsum("cqhd,cqhd->chq", grad_blocks, attended, preferred_element_type=jnp.float32)[
        ..., None
    ]
    grad_scores = (probs * (dprobs - delta) * score_scale).astype(jnp.bfloat16)
    grad_query = jnp.einsum(
        "chqk,ckhd->cqhd", grad_scores, key_windows, preferred_element_type=jnp.float32
    )
    grad_key_win = jnp.einsum(
        "chqk,cqhd->ckhd", grad_scores, query_blocks, preferred_element_type=jnp.float32
    )
    grad_value_win = jnp.einsum(
        "chqk,cqhd->ckhd", probs_b, grad_blocks, preferred_element_type=jnp.float32
    )
    grad_key_win = grad_key_win.reshape(block_count, 2 * BLOCK, features)
    grad_value_win = grad_value_win.reshape(block_count, 2 * BLOCK, features)
    back_k, back_v = (
        shifted(grad_key_win[0, :BLOCK].astype(jnp.bfloat16), "seq", -1).astype(jnp.float32),
        shifted(grad_value_win[0, :BLOCK].astype(jnp.bfloat16), "seq", -1).astype(jnp.float32),
    )
    grad_keys = grad_key_win[:, BLOCK:] + jnp.concatenate(
        [grad_key_win[1:, :BLOCK], back_k[None]], axis=0
    )
    grad_values = grad_value_win[:, BLOCK:] + jnp.concatenate(
        [grad_value_win[1:, :BLOCK], back_v[None]], axis=0
    )
    attended_rows = attended.reshape(frames, features)
    grad_out_weight = lax.psum_scatter(
        lax.dot_general(
            attended_rows, grad_hidden, (((0,), (0,)), ((), ())), preferred_element_type=jnp.float32
        ),
        "seq",
        scatter_dimension=0,
        tiled=True,
    )
    return (
        grad_query.reshape(frames, features).astype(jnp.bfloat16),
        grad_keys.reshape(frames, features).astype(jnp.bfloat16),
        grad_values.reshape(frames, features).astype(jnp.bfloat16),
        grad_hidden,
        grad_out_weight,
        grad_conv_weight,
    )


def solution(mesh):
    in_specs = (
        P(("groups", "seq"), None),
        P(("groups", "seq"), None),
        P(("groups", "seq"), None),
        P(("groups", "seq"), None),
        P(),
        P(),
        P(("groups", "seq"), None),
        P(("groups", "seq")),
    )
    out_specs = (
        P(("groups", "seq"), None),
        P(("groups", "seq"), None),
        P(("groups", "seq"), None),
        P(("groups", "seq"), None),
        P(("groups", "seq"), None),
        P("groups", None),
    )
    return jax.shard_map(
        per_device, mesh=mesh, in_specs=in_specs, out_specs=out_specs, check_vma=False
    )
```

profile of v0, /device:TPU:0, one launch (start us, length us, event | category | flops | bytes accessed | tf_op | source)
XLA Modules:
  0.0 362.7 jit_solution(15127257114367143157)
XLA Ops:
  11.3 3.9 %collective-permute-start = (bf16[128,1536]{1,0:T(8,128)(2,1)}, bf16[128,1536]{1,0:T(8,128)(2,1)}, u32[]{:S(2)}, u32[]{:S(2)}) collective-permute-start(bf16[128,1536]{1,0:T(8,128)(2,1)} %slice.330), channel_id=1, source_target_pairs={{0,1},{1,2},{2,3},{3,4},{4,5},{5,6},{6,7},{7,8},{8,9},{9,10},{10,1... | collective-permute-start | bytes 1179656 | tf_op jit(solution)/shard_map/ppermute | solution.py:16
  17.0 4.5 %collective-permute-start.2 = (bf16[128,1536]{1,0:T(8,128)(2,1)}, bf16[128,1536]{1,0:T(8,128)(2,1)}, u32[]{:S(2)}, u32[]{:S(2)}) collective-permute-start(bf16[128,1536]{1,0:T(8,128)(2,1)} %slice.396), channel_id=1, source_target_pairs={{0,1},{1,2},{2,3},{3,4},{4,5},{5,6},{6,7},{7,8},{8,9},{9,10},{10,1... | collective-permute-start | bytes 1179656 | tf_op jit(solution)/shard_map/ppermute | solution.py:16
  22.4 2.3 collective-permute-start.5
  24.8 3.5 convert_element_type.65
  30.0 2.8 reshape.102
  32.7 2.7 reshape.104
  37.2 4.4 %reshape.106 = bf16[4,128,16,96]{3,2,1,0:T(8,128)(2,1)} reshape(bf16[512,1536]{1,0:T(8,128)(2,1)} %param.8) | data formatting | bytes 3145728 | tf_op jit(solution)/shard_map/reshape | solution.py:71
  41.6 4.4 %copy.30 = bf16[4,128,16,96]{1,3,2,0:T(8,128)(2,1)} copy(bf16[4,128,16,96]{3,2,1,0:T(8,128)(2,1)} %reshape.106) | data formatting | bytes 3145728 | tf_op jit(solution)/shard_map/reshape | solution.py:71
  46.1 4.5 %copy.28 = bf16[4,128,16,96]{1,3,2,0:T(8,128)(2,1)} copy(bf16[4,128,16,96]{3,2,1,0:T(8,128)(2,1)} %reshape.102) | data formatting | bytes 3145728 | tf_op jit(solution)/shard_map/reshape | solution.py:22
  50.5 4.4 %copy.35 = bf16[4,128,16,96]{1,3,2,0:T(8,128)(2,1)} copy(bf16[4,128,16,96]{3,2,1,0:T(8,128)(2,1)} %reshape.104) | data formatting | bytes 3145728 | tf_op jit(solution)/shard_map/reshape | solution.py:22
  56.5 6.1 %fusion.63 = (f32[1536]{0:T(1024)}, f32[1536]{0:T(1024)}, f32[1536]{0:T(1024)}, f32[1536]{0:T(1024)}, f32[1536]{0:T(1024)}, /*index=5*/f32[1536]{0:T(1024)}, f32[1536]{0:T(1024)}, f32[1536]{0:T(1024)}, f32[1536]{0:T(1024)}) fusion(bf16[512,1536]{1,0:T(8,128)(2,1)} %param.14, f32[30,1536]{1,0:T(8,128)S(1)} %convert_element_type.83, ...), kind=kLoop, calls=%fused_computation.156 | loop fusion | flops 22006272 | bytes 4958208 | tf_op jit(solution)/shard_map/reduce_sum | solution.py:53
  62.6 4.5 %fusion.62 = (f32[1536]{0:T(1024)}, f32[1536]{0:T(1024)}, f32[1536]{0:T(1024)}, f32[1536]{0:T(1024)}, f32[1536]{0:T(1024)}, /*index=5*/f32[1536]{0:T(1024)}, f32[1536]{0:T(1024)}, f32[1536]{0:T(1024)}, f32[1536]{0:T(1024)}) fusion(bf16[512,1536]{1,0:T(8,128)(2,1)S(1)} %copy-done, f32[30,1536]{1,0:T(8,128)S(1)} %convert_element_type.83, ...), kind=kLoop, calls=%fused_computation.155 | loop fusion | flops 22006272 | bytes 4958208 | tf_op jit(solution)/shard_map/reduce_sum | solution.py:53
  67.4 4.4 %fusion.64 = (f32[1536]{0:T(1024)}, f32[1536]{0:T(1024)}, f32[1536]{0:T(1024)}, f32[1536]{0:T(1024)}, f32[1536]{0:T(1024)}, /*index=5*/f32[1536]{0:T(1024)}, f32[1536]{0:T(1024)}, f32[1536]{0:T(1024)}, f32[1536]{0:T(1024)}) fusion(bf16[512,1536]{1,0:T(8,128)(2,1)S(1)} %copy-done, f32[512,1536]{1,0:T(8,128)S(1)} %convert_element_type.82, ...), kind=kLoop, calls=%fused_computation.157 | loop fusion | flops 22006272 | bytes 4958208 | tf_op jit(solution)/shard_map/reduce_sum | solution.py:53
  72.1 59.4 %fusion.98 = bf16[512,1536]{1,0:T(8,128)(2,1)} fusion(f32[30,1536]{1,0:T(8,128)S(1)} %convert_element_type.66, f32[512,1536]{1,0:T(8,128)} %convert_element_type.65, bf16[512,1536]{1,0:T(8,128)(2,1)S(1)} %copy-done, f32[1536]{0:T(1024)S(1)} %get-tuple-element.44, f32[1536]{0:T(1024)S(1)} %copy-done.18, f32[1536]{0:T(1024)S(1)} %copy-done.19, ...), kind=kLoop, calls=%fused_computation.191 | loop fusion | flops 73138176 | bytes 6666240 | tf_op jit(solution)/shard_map/convert_element_type | solution.py:46
  131.6 6.7 %convolution_convert_fusion = bf16[512,1536]{1,0:T(8,128)(2,1)} fusion(bf16[512,1536]{1,0:T(8,128)(2,1)} %fusion.98, bf16[1536,1536]{1,0:T(8,128)(2,1)} %param.12), kind=kOutput, calls=%fused_computation.277 | convolution fusion | flops 2416705536 | bytes 7864320 | tf_op jit(solution)/shard_map/dot_general | solution.py:56
  145.1 2.8 stack.127
  150.2 4.5 %reshape.101 = bf16[4,128,16,96]{3,2,1,0:T(8,128)(2,1)} reshape(bf16[512,1536]{1,0:T(8,128)(2,1)} %pad_maximum_fusion.9) | data formatting | bytes 3145728 | tf_op jit(solution)/shard_map/reshape | solution.py:21
  154.7 4.4 %copy.27 = bf16[4,128,16,96]{1,3,2,0:T(8,128)(2,1)} copy(bf16[4,128,16,96]{3,2,1,0:T(8,128)(2,1)} %reshape.101) | data formatting | bytes 3145728 | tf_op jit(solution)/shard_map/reshape | solution.py:21
  161.5 4.5 %reshape.103 = bf16[4,128,16,96]{3,2,1,0:T(8,128)(2,1)} reshape(bf16[512,1536]{1,0:T(8,128)(2,1)} %pad_maximum_fusion.8) | data formatting | bytes 3145728 | tf_op jit(solution)/shard_map/reshape | solution.py:21
  165.9 4.5 %copy.34 = bf16[4,128,16,96]{1,3,2,0:T(8,128)(2,1)} copy(bf16[4,128,16,96]{3,2,1,0:T(8,128)(2,1)} %reshape.103) | data formatting | bytes 3145728 | tf_op jit(solution)/shard_map/reshape | solution.py:21
  170.4 11.1 %bitcast_reduce_fusion = (f32[4,16,128]{2,1,0:T(8,128)S(1)}, f32[4,16,256,128]{3,2,1,0:T(8,128)}) fusion(pred[4,256]{1,0:T(4,128)(4,1)S(1)} %copy-done.75, bf16[4,128,16,96]{1,3,2,0:T(8,128)(2,1)S(1)} %copy-done.10, bf16[4,128,16,96]{1,3,2,0:T(8,128)(2,1)} %copy.28, bf16[4,128,16,96]{1,3,2,0:T(8,128)(2,1)} %copy.27), kind=kOutput, calls=%fused_computation.92 | convolution fusion | flops 830472448 | bytes 13140992 | tf_op jit(solution)/shard_map/sub | solution.py:79
  181.6 4.8 %fusion.8 = bf16[4,16,128,256]{2,3,1,0:T(8,128)(2,1)S(1)} fusion(f32[4,16,128]{2,1,0:T(8,128)S(1)} %get-tuple-element.74, f32[4,16,256,128]{3,2,1,0:T(8,128)} %get-tuple-element.75), kind=kLoop, calls=%fused_computation.101 | loop fusion | flops 4194304 | bytes 12615680 | tf_op jit(solution)/shard_map/convert_element_type | solution.py:81
  190.2 5.0 %fusion.165 = f32[1536,1536]{1,0:T(8,128)} fusion(bf16[512,1536]{1,0:T(8,128)(2,1)S(1)} %copy-done.16, bf16[192,8,4,128]{3,2,1,0:T(4,128)(2,1)S(1)} %bitcast.66), kind=kOutput, calls=%fused_computation.282 | convolution fusion | flops 2415919104 | bytes 12582912 | tf_op jit(solution)/shard_map/dot_general | solution.py:115
  195.3 6.9 %multiply_convert_fusion = bf16[4,16,128,256]{2,3,1,0:T(8,128)(2,1)S(1)} fusion(f32[4,16,128]{2,1,0:T(8,128)S(1)} %get-tuple-element.76, f32[4,16,128]{2,1,0:T(8,128)S(1)} %get-tuple-element.74, f32[4,16,256,128]{3,2,1,0:T(8,128)} %get-tuple-element.75, bf16[4,128,16,96]{1,3,2,0:T(8,128)(2,1)} %copy.35, bf16[4,128,16,96]{1,3,2,0:T(8,128)(2,1)} %copy.34, ...), kind=kOutput, calls=%fused_computation.93 | convolution fusion | flops 419430400 | bytes 17367040 | tf_op jit(solution)/shard_map/cqhd,ckhd->chqk/dot_general | solution.py:85
  206.4 4.4 %copy.68 = bf16[4,128,16,96]{3,2,1,0:T(8,128)(2,1)} copy(bf16[4,128,16,96]{1,3,2,0:T(8,128)(2,1)} %fusion.168) | data formatting | bytes 3145728
  210.8 4.6 %reshape.105 = bf16[512,1536]{1,0:T(8,128)(2,1)} reshape(bf16[4,128,16,96]{3,2,1,0:T(8,128)(2,1)} %copy.68) | data formatting | bytes 3145728
  215.5 3.7 %fusion.185 = f32[4,16,256,96]{2,3,1,0:T(8,128)S(1)} fusion(bf16[4,16,128,256]{2,3,1,0:T(8,128)(2,1)} %copy-done.13, bf16[4,128,16,96]{1,3,2,0:T(8,128)(2,1)S(1)} %copy-done.10), kind=kOutput, calls=%fused_computation.340 | convolution fusion | flops 402653184 | bytes 12058624 | tf_op jit(solution)/shard_map/chqk,cqhd->ckhd/dot_general | solution.py:95
  227.0 2.6 copy.43
  229.7 3.4 fusion.158
  233.0 2.6 copy.46
  235.6 3.7 %all-reduce.3.cloned.1.call-done = f32[31,1536]{1,0:T(8,128)} async-done(((f32[31,1536]{1,0:T(8,128)}), f32[31,1536]{1,0:T(8,128)}) %all-reduce.3.cloned.1.call-update) | async-done | bytes 190480 | tf_op jit(solution)/shard_map/psum | solution.py:55
  239.3 114.9 %reduce-scatter.2.cloned.1.call-done = f32[96,1536]{1,0:T(8,128)} async-done(((f32[1536,1536]{1,0:T(8,128)}), f32[96,1536]{1,0:T(8,128)}) %reduce-scatter.2.cloned.1.call-update) | async-done | bytes 589840 | tf_op jit(solution)/shard_map/reduce_scatter | solution.py:114
  (226 shorter events, 40.4 us)
Async XLA Ops:
  7.2 232.2 %all-reduce.3.cloned.1.call-start = ((), (), s32[]{:S(2)}) async-start(), calls=%async_computation.2 | async-start | bytes 393216 | tf_op jit(solution)/shard_map/psum | solution.py:55
  8.1 20.1 %copy-start.17 = (bf16[31,1536]{1,0:T(8,128)(2,1)S(1)}, bf16[31,1536]{1,0:T(8,128)(2,1)}, u32[]{:S(2)}) copy-start(bf16[31,1536]{1,0:T(8,128)(2,1)} %param.13) | copy-start | bytes 285700
  8.1 63.7 %collective-permute-start.1 = (bf16[30,1536]{1,0:T(8,128)(2,1)S(1)}, bf16[30,1536]{1,0:T(8,128)(2,1)S(1)}, u32[]{:S(2)}, u32[]{:S(2)}) collective-permute-start(bf16[30,1536]{1,0:T(8,128)(2,1)S(1)} %slice.336), channel_id=1, source_target_pairs={{1,0},{2,1},{3,2},{4,3},{5,4},{6,5},{7,6},{8,7},{9,8},{10,9},{11,1... | collective-permute-start | bytes 276488 | tf_op jit(solution)/shard_map/ppermute | solution.py:16
  11.3 18.6 %copy-start.5 = (bf16[512,1536]{1,0:T(8,128)(2,1)S(1)}, bf16[512,1536]{1,0:T(8,128)(2,1)}, u32[]{:S(2)}) copy-start(bf16[512,1536]{1,0:T(8,128)(2,1)} %param.9) | copy-start | bytes 4718596
  11.3 136.7 %collective-permute-start = (bf16[128,1536]{1,0:T(8,128)(2,1)}, bf16[128,1536]{1,0:T(8,128)(2,1)}, u32[]{:S(2)}, u32[]{:S(2)}) collective-permute-start(bf16[128,1536]{1,0:T(8,128)(2,1)} %slice.330), channel_id=1, source_target_pairs={{0,1},{1,2},{2,3},{3,4},{4,5},{5,6},{6,7},{7,8},{8,9},{9,10},{10,1... | collective-permute-start | bytes 1179656 | tf_op jit(solution)/shard_map/ppermute | solution.py:16
  17.0 142.2 %collective-permute-start.2 = (bf16[128,1536]{1,0:T(8,128)(2,1)}, bf16[128,1536]{1,0:T(8,128)(2,1)}, u32[]{:S(2)}, u32[]{:S(2)}) collective-permute-start(bf16[128,1536]{1,0:T(8,128)(2,1)} %slice.396), channel_id=1, source_target_pairs={{0,1},{1,2},{2,3},{3,4},{4,5},{5,6},{6,7},{7,8},{8,9},{9,10},{10,1... | collective-permute-start | bytes 1179656 | tf_op jit(solution)/shard_map/ppermute | solution.py:16
  22.4 33.2 %collective-permute-start.5 = (bf16[30,1536]{1,0:T(8,128)(2,1)S(1)}, bf16[30,1536]{1,0:T(8,128)(2,1)}, u32[]{:S(2)}, u32[]{:S(2)}) collective-permute-start(bf16[30,1536]{1,0:T(8,128)(2,1)S(1)} %slice.404), channel_id=1, source_target_pairs={{0,1},{1,2},{2,3},{3,4},{4,5},{5,6},{6,7},{7,8},{8,9},{9,10},{10,1... | collective-permute-start | bytes 276488 | tf_op jit(solution)/shard_map/ppermute | solution.py:16
  46.1 8.9 %copy-start.74 = (s32[512]{0:T(512)S(1)}, s32[512]{0:T(512)}, u32[]{:S(2)}) copy-start(s32[512]{0:T(512)} %param.15) | copy-start | bytes 6148
  55.0 7.6 %copy-start = (bf16[512,1536]{1,0:T(8,128)(2,1)S(1)}, bf16[512,1536]{1,0:T(8,128)(2,1)}, u32[]{:S(2)}) copy-start(bf16[512,1536]{1,0:T(8,128)(2,1)} %param.14) | copy-start | bytes 4718596
  67.1 4.8 %copy-start.23 = (f32[1536]{0:T(1024)S(1)}, f32[1536]{0:T(1024)}, u32[]{:S(2)}) copy-start(f32[1536]{0:T(1024)} %get-tuple-element.50) | copy-start | bytes 18436
  67.1 4.8 %copy-start.24 = (f32[1536]{0:T(1024)S(1)}, f32[1536]{0:T(1024)}, u32[]{:S(2)}) copy-start(f32[1536]{0:T(1024)} %get-tuple-element.51) | copy-start | bytes 18436
  67.1 4.8 %copy-start.25 = (f32[1536]{0:T(1024)S(1)}, f32[1536]{0:T(1024)}, u32[]{:S(2)}) copy-start(f32[1536]{0:T(1024)} %get-tuple-element.52) | copy-start | bytes 18436
  67.1 4.8 %copy-start.26 = (f32[1536]{0:T(1024)S(1)}, f32[1536]{0:T(1024)}, u32[]{:S(2)}) copy-start(f32[1536]{0:T(1024)} %get-tuple-element.53) | copy-start | bytes 18436
  67.2 4.8 %copy-start.27 = (f32[1536]{0:T(1024)S(1)}, f32[1536]{0:T(1024)}, u32[]{:S(2)}) copy-start(f32[1536]{0:T(1024)} %get-tuple-element.54) | copy-start | bytes 18436
  67.2 4.8 %copy-start.28 = (f32[1536]{0:T(1024)S(1)}, f32[1536]{0:T(1024)}, u32[]{:S(2)}) copy-start(f32[1536]{0:T(1024)} %get-tuple-element.55) | copy-start | bytes 18436
  67.2 4.8 %copy-start.29 = (f32[1536]{0:T(1024)S(1)}, f32[1536]{0:T(1024)}, u32[]{:S(2)}) copy-start(f32[1536]{0:T(1024)} %get-tuple-element.56) | copy-start | bytes 18436
  67.2 4.8 %copy-start.30 = (f32[1536]{0:T(1024)S(1)}, f32[1536]{0:T(1024)}, u32[]{:S(2)}) copy-start(f32[1536]{0:T(1024)} %get-tuple-element.57) | copy-start | bytes 18436
  67.2 4.8 %copy-start.31 = (f32[1536]{0:T(1024)S(1)}, f32[1536]{0:T(1024)}, u32[]{:S(2)}) copy-start(f32[1536]{0:T(1024)} %get-tuple-element.58) | copy-start | bytes 18436
  67.2 4.8 %copy-start.32 = (f32[1536]{0:T(1024)S(1)}, f32[1536]{0:T(1024)}, u32[]{:S(2)}) copy-start(f32[1536]{0:T(1024)} %get-tuple-element.59) | copy-start | bytes 18436
  131.6 6.7 %copy-start.9 = (bf16[512,1536]{1,0:T(8,128)(2,1)S(1)}, bf16[512,1536]{1,0:T(8,128)(2,1)}, u32[]{:S(2)}) copy-start(bf16[512,1536]{1,0:T(8,128)(2,1)} %param.11) | copy-start | bytes 4718596
  142.5 5.5 %copy-start.6 = (bf16[512,1536]{1,0:T(8,128)(2,1)S(1)}, bf16[512,1536]{1,0:T(8,128)(2,1)}, u32[]{:S(2)}) copy-start(bf16[512,1536]{1,0:T(8,128)(2,1)} %param.9) | copy-start | bytes 4718596
  147.9 206.3 %reduce-scatter.2.cloned.1.call-start = ((), (), s32[]{:S(2)}) async-start(), calls=%async_computation.1 | async-start | bytes 10027008 | tf_op jit(solution)/shard_map/reduce_scatter | solution.py:114
  150.2 8.9 %copy-start.8 = (bf16[512,1536]{1,0:T(8,128)(2,1)S(1)}, bf16[512,1536]{1,0:T(8,128)(2,1)}, u32[]{:S(2)}) copy-start(bf16[512,1536]{1,0:T(8,128)(2,1)} %param.10) | copy-start | bytes 4718596
  161.5 8.9 %copy-start.10 = (bf16[4,128,16,96]{1,3,2,0:T(8,128)(2,1)S(1)}, bf16[4,128,16,96]{1,3,2,0:T(8,128)(2,1)}, u32[]{:S(2)}) copy-start(bf16[4,128,16,96]{1,3,2,0:T(8,128)(2,1)} %copy.30) | copy-start | bytes 4718596
  161.5 8.9 %copy-start.75 = (pred[4,256]{1,0:T(4,128)(4,1)S(1)}, pred[4,256]{1,0:T(4,128)(4,1)}, u32[]{:S(2)}) copy-start(pred[4,256]{1,0:T(4,128)(4,1)} %add_compare_fusion) | copy-start | bytes 3076
  181.6 4.8 %copy-start.4 = (f32[4,16,128,96]{2,0,3,1:T(4,128)S(1)}, f32[4,16,128,96]{2,0,3,1:T(4,128)}, u32[]{:S(2)}) copy-start(f32[4,16,128,96]{2,0,3,1:T(4,128)} %bitcast_convert_fusion) | copy-start | bytes 9437188
  181.6 4.8 %copy-start.11 = (bf16[4,128,16,96]{1,3,2,0:T(8,128)(2,1)S(1)}, bf16[4,128,16,96]{1,3,2,0:T(8,128)(2,1)}, u32[]{:S(2)}) copy-start(bf16[4,128,16,96]{1,3,2,0:T(8,128)(2,1)} %copy.35) | copy-start | bytes 4718596
  181.6 5.2 %copy-start.12 = (bf16[4,128,16,96]{1,3,2,0:T(8,128)(2,1)S(1)}, bf16[4,128,16,96]{1,3,2,0:T(8,128)(2,1)}, u32[]{:S(2)}) copy-start(bf16[4,128,16,96]{1,3,2,0:T(8,128)(2,1)} %copy.34) | copy-start | bytes 4718596
  195.3 9.0 %copy-start.14 = (bf16[4,128,16,96]{1,3,2,0:T(8,128)(2,1)S(1)}, bf16[4,128,16,96]{1,3,2,0:T(8,128)(2,1)}, u32[]{:S(2)}) copy-start(bf16[4,128,16,96]{1,3,2,0:T(8,128)(2,1)} %copy.28) | copy-start | bytes 4718596
  195.3 9.0 %copy-start.15 = (bf16[4,128,16,96]{1,3,2,0:T(8,128)(2,1)S(1)}, bf16[4,128,16,96]{1,3,2,0:T(8,128)(2,1)}, u32[]{:S(2)}) copy-start(bf16[4,128,16,96]{1,3,2,0:T(8,128)(2,1)} %copy.27) | copy-start | bytes 4718596
  219.4 5.0 %collective-permute-start.3 = (bf16[128,1536]{0,1:T(8,128)(2,1)S(1)}, bf16[128,1536]{0,1:T(8,128)(2,1)S(1)}, u32[]{:S(2)}, u32[]{:S(2)}) collective-permute-start(bf16[128,1536]{0,1:T(8,128)(2,1)S(1)} %fusion.173), channel_id=1, source_target_pairs={{1,0},{2,1},{3,2},{4,3},{5,4},{6,5},{7,6},{8,7},{9,8},{10,9},{11,1... | collective-permute-start | bytes 1179656 | tf_op jit(solution)/shard_map/ppermute | solution.py:16
  223.1 6.5 %collective-permute-start.4 = (bf16[128,1536]{0,1:T(8,128)(2,1)S(1)}, bf16[128,1536]{0,1:T(8,128)(2,1)S(1)}, u32[]{:S(2)}, u32[]{:S(2)}) collective-permute-start(bf16[128,1536]{0,1:T(8,128)(2,1)S(1)} %fusion.174), channel_id=1, source_target_pairs={{1,0},{2,1},{3,2},{4,3},{5,4},{6,5},{7,6},{8,7},{9,8},{10,9},{11,1... | collective-permute-start | bytes 1179656 | tf_op jit(solution)/shard_map/ppermute | solution.py:16
  (52 other events, 171.5 us)
Sparse Core Ops, SparseCore 0:
  148.1 91.2 all-reduce.2
  244.0 110.1 reduce-scatter.1
where the time goes:
time: 364 us; the launch traced here: 363 us
  waiting for transfers between devices  119 us (33%)
  other arithmetic  99.3 us (27%)
  local copies, waits for them, and re-layouts  75.9 us (21%)
  matrix products  38.3 us (11%)
  between operations  15.4 us (4%)
  starting transfers between devices  15.1 us (4%)
    reduce_scatter x1, waiting for transfers between devices, per_device(): lax.psum_scatter(lax.dot_general(attended_rows, grad_hidden, (((0,), (0,)...  115 us
    convert_element_type x1, other arithmetic, per_device(): grad_hidden = running.astype(jnp.bfloat16)  59.4 us
    reshape x4, local copies, waits for them, and re-layouts, window_of(): earlier = extended[:frames].reshape((block_count, BLOCK) + tail_shape)  17.9 us
    reduce_sum x4, other arithmetic, per_device(): jnp.sum(hidden_pad[rim_rows - offset:rim_rows - offset + frames] * upstre...  16.8 us
    unnamed x155, local copies, waits for them, and re-layouts  15.9 us
    ppermute x6, starting transfers between devices, shifted(): lax.ppermute(value, axis, [(source, source + steps) for source in range(i...  15 us
    reshape x4, local copies, waits for them, and re-layouts, window_of(): current = extended[BLOCK:].reshape((block_count, BLOCK) + tail_shape)  14.4 us
    sub x1, matrix products, per_device(): weights_raw = jnp.where(allowed, jnp.exp(scores - row_max), 0.0)  11.1 us
  transfers between devices with their start and end apart: 8, of which 2 were waited for; matrix products, arithmetic and copies ran while one was open for 57% of the time, Pallas kernels for 0%

commit v1 on v0

v1 whole, which is shorter than its diff:
```python
import math

import jax
import jax.numpy as jnp
from jax import lax
from jax.experimental import pallas as pl
from jax.experimental.pallas import tpu as pltpu
from jax.sharding import PartitionSpec as P

HEADS = 16
KERNEL = 31
BLOCK = 128
LANES = 128
HALO = 32
CHUNK = 64
AXIS = "seq"
F32 = jnp.float32
BF16 = jnp.bfloat16


def shifted(value, steps):
    count = lax.axis_size(AXIS)
    initial, last = (max(0, -steps), min(count, count - steps))
    return lax.ppermute(value, AXIS, [(s, s + steps) for s in range(initial, last)])


def exchanged(value, bit):
    count = lax.axis_size(AXIS)
    return lax.ppermute(value, AXIS, [(i, i ^ (1 << bit)) for i in range(count)])


def dot(a, b, ca, cb):
    return lax.dot_general(a, b, (((ca,), (cb,)), ((), ())), preferred_element_type=F32)


def conv_kernel(cot_ref, next_ref, hid_ref, taps_ref, gh_ref, gw_ref, cs, wb, acc_w):
    rows, width = cot_ref.shape
    for tile in range(width // LANES):
        lanes = slice(tile * LANES, (tile + 1) * LANES)
        cs[:rows, :] = cot_ref[:, lanes].astype(F32)
        cs[rows:, :] = next_ref[:, lanes].astype(F32)
        taps = taps_ref[:, lanes].astype(F32)
        for m in range(KERNEL):
            wb[m] = jnp.broadcast_to(taps[m : m + 1], (8, LANES))
        acc_w[...] = jnp.zeros_like(acc_w)

        def step(i, carry, lanes=lanes):
            base = pl.multiple_of(i * CHUNK, CHUNK)
            count = CHUNK // 8
            hid = hid_ref[pl.ds(base, CHUNK), lanes].astype(F32)
            hid = [hid[8 * j : 8 * j + 8] for j in range(count)]
            out = [None] * count
            for r in range(8):
                offsets = list(range(r, KERNEL, 8))
                c = [cs[pl.ds(base + r + 8 * j, 8), :] for j in range(count + len(offsets) - 1)]
                for a, m in enumerate(offsets):
                    tap = wb[m]
                    prods = []
                    for j in range(count):
                        term = tap * c[j + a]
                        out[j] = term if out[j] is None else out[j] + term
                        prods.append(hid[j] * c[j + a])
                    while len(prods) > 1:
                        prods = [prods[k] + prods[k + 1] for k in range(0, len(prods), 2)]
                    acc_w[m] += prods[0]
            gh_ref[pl.ds(base, CHUNK), lanes] = jnp.concatenate(out, axis=0).astype(BF16)
            return carry

        lax.fori_loop(0, rows // CHUNK, step, 0)
        gw_ref[:KERNEL, lanes] = jnp.sum(acc_w[...], axis=1).astype(BF16)
        gw_ref[KERNEL:, lanes] = jnp.zeros((gw_ref.shape[0] - KERNEL, LANES), BF16)


def convolution(cotangent, cot_next, hidden, conv_weight):
    rows, features = cotangent.shape
    width = 3 * LANES
    col = lambda g: (0, g)
    return pl.pallas_call(
        conv_kernel,
        name="conv",
        grid=(features // width,),
        in_specs=[
            pl.BlockSpec((rows, width), col),
            pl.BlockSpec((HALO, width), col),
            pl.BlockSpec((rows, width), col),
            pl.BlockSpec((KERNEL, width), col),
        ],
        out_specs=[pl.BlockSpec((rows, width), col), pl.BlockSpec((HALO, width), col)],
        out_shape=[
            jax.ShapeDtypeStruct((rows, features), BF16),
            jax.ShapeDtypeStruct((HALO, features), BF16),
        ],
        scratch_shapes=[
            pltpu.VMEM((rows + HALO, LANES), F32),
            pltpu.VMEM((KERNEL, 8, LANES), F32),
            pltpu.VMEM((KERNEL, 8, LANES), F32),
        ],
    )(cotangent, cot_next, hidden, conv_weight)


def pair_masks(pair, head, dtype):
    at = lax.broadcasted_iota(jnp.int32, (1, 2 * LANES), 1)
    low = pair * (2 * head - LANES)
    first = (at >= low) & (at < low + head)
    second = (at >= low + head) & (at < low + 2 * head)
    return first.astype(F32).astype(dtype), second.astype(F32).astype(dtype)


def window(pair):
    return slice(pair * LANES, pair * LANES + 2 * LANES)


def key_window(ctx_ref, which, ref, b, pair):
    win = window(pair)
    if b == 0:
        return jnp.concatenate([ctx_ref[which, :, win], ref[:BLOCK, win]], axis=0)
    return ref[(b - 1) * BLOCK : (b + 1) * BLOCK, win]


def stacked(ref, b, pair, masks):
    rows = ref[b * BLOCK : (b + 1) * BLOCK, window(pair)]
    return jnp.concatenate([rows * masks[0], rows * masks[1]], axis=0)


def forward_kernel(q_ref, k_ref, v_ref, ctx_ref, bias_ref, att_ref, p_ref):
    rows, width = q_ref.shape
    head = width // 4
    factor = math.log2(math.e) / math.sqrt(head)
    for pair in range(2):
        masks = pair_masks(pair, head, BF16)
        low = pair * (2 * head - LANES)
        for b in range(rows // BLOCK):
            keys = key_window(ctx_ref, 0, k_ref, b, pair)
            values = key_window(ctx_ref, 1, v_ref, b, pair)
            bias = bias_ref[b * BLOCK : (b + 2) * BLOCK, :]
            scores = dot(keys, stacked(q_ref, b, pair, masks), 1, 1)
            scores = scores * factor + jnp.concatenate([bias, bias], axis=1)
            top = jnp.max(scores, axis=0, keepdims=True)
            weights = jnp.exp2(scores - top)
            total = jnp.sum(weights, axis=0, keepdims=True)
            probs = (weights * (1.0 / total)).astype(BF16)
            p_ref[b, pair] = probs
            out = dot(values, probs, 0, 0).astype(BF16)
            cols = slice(b * BLOCK, (b + 1) * BLOCK)
            at = 2 * head * pair
            att_ref[at : at + head, cols] = out[low : low + head, :BLOCK]
            att_ref[at + head : at + 2 * head, cols] = out[low + head : low + 2 * head, BLOCK:]


def forward_attention(queries, keys, values, context, bias):
    rows, features = queries.shape
    width = 4 * (features // HEADS)
    assert width == 3 * LANES
    blocks = rows // BLOCK
    col = lambda g: (0, g)
    return pl.pallas_call(
        forward_kernel,
        name="forward",
        grid=(features // width,),
        in_specs=[
            pl.BlockSpec((rows, width), col),
            pl.BlockSpec((rows, width), col),
            pl.BlockSpec((rows, width), col),
            pl.BlockSpec((2, BLOCK, width), lambda g: (0, 0, g)),
            pl.BlockSpec((rows + BLOCK, LANES), lambda g: (0, 0)),
        ],
        out_specs=[
            pl.BlockSpec((width, rows), lambda g: (g, 0)),
            pl.BlockSpec((blocks, 2, 2 * BLOCK, 2 * BLOCK), lambda g: (0, g, 0, 0)),
        ],
        out_shape=[
            jax.ShapeDtypeStruct((features, rows), BF16),
            jax.ShapeDtypeStruct((blocks, HEADS // 2, 2 * BLOCK, 2 * BLOCK), BF16),
        ],
    )(queries, keys, values, context, bias)


def backward_kernel(
    gh_ref, w_ref, q_ref, k_ref, v_ref, ctx_ref, p_ref, gq_ref, gk_ref, gv_ref, back_ref, last_ref, ga
):
    rows, width = q_ref.shape
    head = width // 4
    scale = 1.0 / math.sqrt(head)
    blocks = rows // BLOCK
    ga[...] = dot(gh_ref[...], w_ref[...], 1, 1).astype(BF16)

    def merged(parts):
        first, second = parts
        return jnp.concatenate(
            [first[:, :LANES], first[:, LANES:] + second[:, :LANES], second[:, LANES:]], axis=1
        )

    above_k = above_v = None
    for b in range(blocks):
        gq, gk, gv = [], [], []
        for pair in range(2):
            masks = pair_masks(pair, head, BF16)
            masks_f = pair_masks(pair, head, F32)
            keys = key_window(ctx_ref, 0, k_ref, b, pair)
            values = key_window(ctx_ref, 1, v_ref, b, pair)
            q2 = stacked(q_ref, b, pair, masks)
            g2 = stacked(ga, b, pair, masks)
            probs = p_ref[b, pair]
            dprobs = dot(values, g2, 1, 1)
            probs_f = probs.astype(F32)
            weighted = probs_f * dprobs
            delta = jnp.sum(weighted, axis=0, keepdims=True)
            dscores = (weighted - probs_f * delta).astype(BF16)
            gv.append(dot(probs, g2, 1, 0))
            gk.append(dot(dscores, q2, 1, 0))
            both = dot(dscores, keys, 0, 0)
            gq.append(both[:BLOCK] * masks_f[0] + both[BLOCK:] * masks_f[1])
        gq_ref[b * BLOCK : (b + 1) * BLOCK, :] = (merged(gq) * scale).astype(BF16)
        gk = merged(gk) * scale
        gv = merged(gv)
        if b == 0:
            back_ref[0] = gk[:BLOCK].astype(BF16)
            back_ref[1] = gv[:BLOCK].astype(BF16)
        else:
            at = slice((b - 1) * BLOCK, b * BLOCK)
            gk_ref[at, :] = (above_k + gk[:BLOCK]).astype(BF16)
            gv_ref[at, :] = (above_v + gv[:BLOCK]).astype(BF16)
        above_k, above_v = gk[BLOCK:], gv[BLOCK:]
    at = slice((blocks - 1) * BLOCK, blocks * BLOCK)
    gk_ref[at, :] = above_k.astype(BF16)
    gv_ref[at, :] = above_v.astype(BF16)
    last_ref[0] = above_k
    last_ref[1] = above_v


def backward_attention(grad_hidden, out_weight, queries, keys, values, context, probs):
    rows, features = queries.shape
    width = 4 * (features // HEADS)
    blocks = rows // BLOCK
    col = lambda g: (0, g)
    rim = pl.BlockSpec((2, BLOCK, width), lambda g: (0, 0, g))
    wide = pl.BlockSpec((rows, width), col)
    return pl.pallas_call(
        backward_kernel,
        name="backward",
        grid=(features // width,),
        in_specs=[
            pl.BlockSpec((rows, features), lambda g: (0, 0)),
            pl.BlockSpec((width, features), lambda g: (g, 0)),
            wide,
            wide,
            wide,
            rim,
            pl.BlockSpec((blocks, 2, 2 * BLOCK, 2 * BLOCK), lambda g: (0, g, 0, 0)),
        ],
        out_specs=[wide, wide, wide, rim, rim],
        out_shape=[
            jax.ShapeDtypeStruct((rows, features), BF16),
            jax.ShapeDtypeStruct((rows, features), BF16),
            jax.ShapeDtypeStruct((rows, features), BF16),
            jax.ShapeDtypeStruct((2, BLOCK, features), BF16),
            jax.ShapeDtypeStruct((2, BLOCK, features), F32),
        ],
        scratch_shapes=[pltpu.VMEM((rows, width), BF16)],
    )(grad_hidden, out_weight, queries, keys, values, context, probs)


def finish_kernel(gk_in, gv_in, last_ref, back_ref, gk_ref, gv_ref):
    gk_ref[...] = (last_ref[0] + back_ref[0].astype(F32)).astype(BF16)
    gv_ref[...] = (last_ref[1] + back_ref[1].astype(F32)).astype(BF16)


def finish(gk, gv, last, back):
    rows, features = gk.shape
    rim = pl.BlockSpec((2, BLOCK, features), lambda i: (0, 0, 0))
    end = pl.BlockSpec((BLOCK, features), lambda i: (rows // BLOCK - 1, 0))
    whole = pl.BlockSpec(memory_space=pl.ANY)
    return pl.pallas_call(
        finish_kernel,
        name="finish",
        grid=(1,),
        in_specs=[whole, whole, rim, rim],
        out_specs=[end, end],
        out_shape=[jax.ShapeDtypeStruct(gk.shape, BF16), jax.ShapeDtypeStruct(gv.shape, BF16)],
        input_output_aliases={0: 0, 1: 1},
    )(gk, gv, last, back)


def place(block, order):
    at = 0
    for bit in order:
        at = 2 * at + ((block >> bit) & 1)
    return at


def partial_kernel(order, bit_ref, att_ref, gh_ref, *refs):
    taps, (keep_ref, send_ref, both) = refs[:-3], refs[-3:]
    count = 1 << len(order)
    features = att_ref.shape[0]
    size = features // count
    step = features // 4
    for part in range(4):
        out = dot(att_ref[part * step : (part + 1) * step, :], gh_ref[...], 1, 0).astype(BF16)
        for i in range(step // size):
            half, at = divmod(place(part * (step // size) + i, order), count // 2)
            both[half, at * size : (at + 1) * size, :] = out[i * size : (i + 1) * size]
    mine = bit_ref[0]
    keep_ref[...] = both[mine]
    send_ref[: features // 2, :] = both[1 - mine]
    for i, ref in enumerate(taps):
        at = features // 2 + i * HALO
        send_ref[at : at + HALO, :] = ref[...]


def partial_product(attended_t, grad_hidden, first_col, cols, order, taps=None):
    features, rows = attended_t.shape
    width = 2 * LANES
    count = 1 << len(order)
    assert cols % width == 0 and (features // 4) % (features // count) == 0
    bit = ((lax.axis_index(AXIS) >> order[0]) & 1).astype(jnp.int32).reshape(1)
    extra, args = [], []
    if taps is not None:
        for part in range(features // cols):
            extra.append(pl.BlockSpec((HALO, width), lambda j, s, part=part: (0, part * (cols // width) + j)))
            args.append(taps)
    height = features // 2 + HALO * len(extra)

    def kernel(*refs):
        partial_kernel(order, *refs)

    return pl.pallas_call(
        kernel,
        name="partial",
        grid_spec=pltpu.PrefetchScalarGridSpec(
            num_scalar_prefetch=1,
            grid=(cols // width,),
            in_specs=[
                pl.BlockSpec((features, rows), lambda j, s: (0, 0)),
                pl.BlockSpec((rows, width), lambda j, s: (0, first_col // width + j)),
                *extra,
            ],
            out_specs=[
                pl.BlockSpec((features // 2, width), lambda j, s: (0, j)),
                pl.BlockSpec((height, width), lambda j, s: (0, j)),
            ],
            scratch_shapes=[pltpu.VMEM((2, features // 2, width), BF16)],
        ),
        out_shape=[
            jax.ShapeDtypeStruct((features // 2, cols), BF16),
            jax.ShapeDtypeStruct((height, cols), BF16),
        ],
    )(bit, attended_t, grad_hidden, *args)


def halves(value, bit):
    mine = (lax.axis_index(AXIS) >> bit) & 1
    value = value.reshape((2, value.shape[0] // 2) + value.shape[1:])
    return (
        lax.dynamic_index_in_dim(value, mine, 0, False),
        lax.dynamic_index_in_dim(value, 1 - mine, 0, False),
    )


def reduce_rows(keep, send, order, taps=None):
    for step, bit in enumerate(order):
        got = exchanged(send, bit)
        rows = keep.shape[0]
        total = keep.astype(F32) + got[:rows].astype(F32)
        if taps is not None:
            taps = taps.astype(BF16).astype(F32) + got[rows:].astype(F32)
        if step + 1 == len(order):
            return total, taps
        keep, send = halves(total.astype(BF16), order[step + 1])
        if taps is not None:
            send = jnp.concatenate([send, taps.astype(BF16)], axis=0)


def per_device(
    queries, key_vectors, value_vectors, hidden, out_weight, conv_weight, cotangent, valid_mask
):
    frames, features = queries.shape
    count = lax.axis_size(AXIS)
    bits = count.bit_length() - 1
    assert count == 1 << bits and bits >= 2
    order_a = list(range(bits))
    order_b = [0, *range(2, bits), 1]

    cot_next = shifted(cotangent[:HALO], -1)
    context = shifted(jnp.stack([key_vectors[frames - BLOCK :], value_vectors[frames - BLOCK :]]), 1)
    grad_hidden, taps = convolution(cotangent, cot_next, hidden, conv_weight)

    has_context = jnp.broadcast_to((lax.axis_index(AXIS) > 0).astype(jnp.int32), (BLOCK,))
    allowed = jnp.concatenate([has_context, valid_mask]) == 1
    bias = jnp.broadcast_to(jnp.where(allowed, 0.0, -1e30).astype(F32)[:, None], (frames + BLOCK, LANES))
    attended_t, probs = forward_attention(queries, key_vectors, value_vectors, context, bias)

    cols = features // 2
    keep_a, send_a = partial_product(attended_t, grad_hidden, 0, cols, order_a)
    keep_b, send_b = partial_product(attended_t, grad_hidden, cols, cols, order_b, taps)
    own_taps = jnp.concatenate([taps[:, :cols], taps[:, cols:]], axis=0)

    gq, gk, gv, back, last = backward_attention(
        grad_hidden, out_weight, queries, key_vectors, value_vectors, context, probs
    )
    gk, gv = finish(gk, gv, last, shifted(back, -1))

    rows_a, _ = reduce_rows(keep_a, send_a, order_a)
    rows_b, sums = reduce_rows(keep_b, send_b, order_b, own_taps)
    grad_out_weight = jnp.concatenate([rows_a, rows_b], axis=1)
    grad_conv_weight = jnp.concatenate([sums[:KERNEL], sums[HALO : HALO + KERNEL]], axis=1)
    return gq, gk, gv, grad_hidden, grad_out_weight, grad_conv_weight


def solution(mesh):
    rows = P(("groups", AXIS), None)
    in_specs = (rows, rows, rows, rows, P(), P(), rows, P(("groups", AXIS)))
    out_specs = (rows, rows, rows, rows, rows, P("groups", None))
    return jax.shard_map(
        per_device, mesh=mesh, in_specs=in_specs, out_specs=out_specs, check_vma=False
    )
```

time: 364 us -> 129 us (0.35)
  waiting for transfers between devices: 119 us -> 25.5 us
  other arithmetic: 99.3 us -> 12.3 us
  local copies, waits for them, and re-layouts: 75.9 us -> 7.67 us
  Pallas kernels: 0 us -> 55.4 us
  matrix products: 38.3 us -> 0 us
  between operations: 15.4 us -> 0.89 us
  starting transfers between devices: 15.1 us -> 26.3 us
    reduce_scatter x1 -> x0, waiting for transfers between devices: 115 us -> none  [per_device(): lax.psum_scatter(lax.dot_general(attended_rows, grad_hidden, (((0,), (0,)...]
    convert_element_type x9, other arithmetic: 75.3 us -> 8.9 us  [the longest x6 7.03 us: reduce_rows(): keep, send = halves(total.astype(BF16), order[step + 1])]
    pallas_call x0 -> x6, Pallas kernels: none -> 55.4 us  [the longest x1 17.2 us: backward_attention(): pl.pallas_call(backward_kernel, name='backward', grid=(features // width,...]
    reshape x11 -> x0, local copies, waits for them, and re-layouts: 41.5 us -> none  [the longest x4 17.9 us: window_of(): earlier = extended[:frames].reshape((block_count, BLOCK) + tail_shape)]
    dot_general x7 -> x0, matrix products: 27.2 us -> none  [the longest x1 6.88 us: per_device(): jnp.einsum('cqhd,ckhd->chqk', grad_blocks, value_windows, preferred_eleme...]
    ppermute x6 -> x11, waiting for transfers between devices: 0.02 us -> 25.5 us  [the longest x8 21.5 us: exchanged(): return lax.ppermute(value, AXIS, [(i, i ^ 1 << bit) for i in range(count)])]
    reduce_sum x4 -> x0, other arithmetic: 16.8 us -> none  [per_device(): jnp.sum(hidden_pad[rim_rows - offset:rim_rows - offset + frames] * upstre...]
    unnamed x155 -> x16, local copies, waits for them, and re-layouts: 15.9 us -> 3.59 us
  transfers between devices with their start and end apart: 8 -> 11, of which waited for: 2 -> 4; matrix products, arithmetic and copies ran while one was open for 57% -> 10% of each run, Pallas kernels for 0% -> 32%
where the time goes in v1:
time: 129 us; the launch traced here: 128 us
  Pallas kernels  55.4 us (43%)
  starting transfers between devices  26.3 us (20%)
  waiting for transfers between devices  25.5 us (20%)
  other arithmetic  12.3 us (10%)
  local copies, waits for them, and re-layouts  7.67 us (6%)
    ppermute x8, waiting for transfers between devices, exchanged(): return lax.ppermute(value, AXIS, [(i, i ^ 1 << bit) for i in range(count)])  21.5 us
    ppermute x8, starting transfers between devices, exchanged(): return lax.ppermute(value, AXIS, [(i, i ^ 1 << bit) for i in range(count)])  21.3 us
    pallas_call x1, Pallas kernels, backward_attention(): pl.pallas_call(backward_kernel, name='backward', grid=(features // width,...  17.2 us
    pallas_call x1, Pallas kernels, convolution(): pl.pallas_call(conv_kernel, name='conv', grid=(features // width,), in_sp...  16.6 us
    pallas_call x2, Pallas kernels, partial_product(): pl.pallas_call(kernel, name='partial', grid_spec=pltpu.PrefetchScalarGrid...  9.86 us
    pallas_call x1, Pallas kernels, forward_attention(): pl.pallas_call(forward_kernel, name='forward', grid=(features // width,),...  9.14 us
    convert_element_type x6, other arithmetic, reduce_rows(): keep, send = halves(total.astype(BF16), order[step + 1])  7.03 us
    ppermute x3, starting transfers between devices, shifted(): lax.ppermute(value, AXIS, [(s, s + steps) for s in range(initial, last)])  5.02 us
  transfers between devices with their start and end apart: 11, of which 4 were waited for; matrix products, arithmetic and copies ran while one was open for 10% of the time, Pallas kernels for 32%

profile of v1, /device:TPU:0, one launch (start us, length us, event | category | flops | bytes accessed | tf_op | source)
XLA Modules:
  0.0 128.1 jit_solution(92027724883830610)
XLA Ops:
  0.6 1.2 slice_bitcast_fusion
  1.9 2.4 %collective-permute-start.1 = (bf16[2,128,1536]{2,1,0:T(8,128)(2,1)S(1)}, bf16[2,128,1536]{2,1,0:T(8,128)(2,1)S(1)}, u32[]{:S(2)}, u32[]{:S(2)}) collective-permute-start(bf16[2,128,1536]{2,1,0:T(8,128)(2,1)S(1)} %pad_maximum_fusion), channel_id=1, source_target_pairs={{0,1},{1,2},{2,3},{3,4},{4,5},{5,6},{6,7},{7,8},{8,9},{9,10},{10,1... | collective-permute-start | bytes 2359304 | tf_op jit(solution)/shard_map/ppermute | solution.py:24
  4.4 0.9 slice.45
  5.3 1.3 collective-permute-start
  6.6 3.9 %collective-permute-done.next_ref = bf16[32,1536]{1,0:T(8,128)(2,1)S(1)} collective-permute-done((bf16[32,1536]{1,0:T(8,128)(2,1)S(1)}, bf16[32,1536]{1,0:T(8,128)(2,1)S(1)}, u32[]{:S(2)}, u32[]{:S(2)}) %collective-permute-start) | collective-permute-done | bytes 98336 | tf_op jit(solution)/shard_map/ppermute | solution.py:24
  11.2 16.6 %conv.1 = (bf16[512,1536]{1,0:T(8,128)(2,1)}, bf16[32,1536]{1,0:T(8,128)(2,1)}) custom-call(bf16[512,1536]{1,0:T(8,128)(2,1)} %cot_ref.1, bf16[32,1536]{1,0:T(8,128)(2,1)} %copy-done.6, bf16[512,1536]{1,0:T(8,128)(2,1)} %hid_ref.1, bf16[31,1536]{1,0:T(8,128)(2,1)} %taps_ref.1), custom_call_target="tpu_custom_call" | custom-call | tf_op jit(solution)/shard_map/conv/pallas_call | solution.py:78
  27.8 1.0 broadcast_in_dim.17.bias_ref
  28.8 9.1 %forward.1 = (bf16[1536,512]{1,0:T(8,128)(2,1)}, bf16[4,8,256,256]{3,2,1,0:T(8,128)(2,1)}) custom-call(bf16[512,1536]{1,0:T(8,128)(2,1)} %q_ref.3, bf16[512,1536]{1,0:T(8,128)(2,1)} %k_ref.3, bf16[512,1536]{1,0:T(8,128)(2,1)} %v_ref.3, bf16[2,128,1536]{2,1,0:T(8,128)(2,1)} %copy-done, f32[640,128]{1,0:T(8,128)} %broadcast_in_dim.17.bias_ref), custom_call_target="tpu_custom_call" | custom-call | tf_op jit(solution)/shard_map/forward/pallas_call | solution.py:156
  37.9 4.9 %partial.2 = (bf16[768,768]{1,0:T(8,128)(2,1)}, bf16[768,768]{1,0:T(8,128)(2,1)}) custom-call(s32[1]{0:T(128)} %bitcast.2.refs_0_, bf16[1536,512]{1,0:T(8,128)(2,1)} %get-tuple-element.30.refs_1_, bf16[512,1536]{1,0:T(8,128)(2,1)} %get-tuple-element.18.gh_ref.refs_2_), custom_call_target="tpu_custom_call" | custom-call | tf_op jit(solution)/shard_map/partial/pallas_call | solution.py:326
  42.8 3.2 %collective-permute-start.3 = (bf16[768,768]{1,0:T(8,128)(2,1)}, bf16[768,768]{1,0:T(8,128)(2,1)S(1)}, u32[]{:S(2)}, u32[]{:S(2)}) collective-permute-start(bf16[768,768]{1,0:T(8,128)(2,1)} %get-tuple-element.32), channel_id=1, source_target_pairs={{0,1},{1,0},{2,3},{3,2},{4,5},{5,4},{6,7},{7,6},{8,9},{9,8},{10,11... | collective-permute-start | bytes 3538952 | tf_op jit(solution)/shard_map/ppermute | solution.py:29
  46.1 5.0 %partial.3 = (bf16[768,768]{1,0:T(8,128)(2,1)}, bf16[832,768]{1,0:T(8,128)(2,1)}) custom-call(s32[1]{0:T(128)} %bitcast.2.refs_0_, bf16[1536,512]{1,0:T(8,128)(2,1)} %get-tuple-element.30.refs_1_, bf16[512,1536]{1,0:T(8,128)(2,1)} %get-tuple-element.18.gh_ref.refs_2_, bf16[32,1536]{1,0:T(8,128)(2,1)} %get-tuple-element.33.refs_3_.refs_4_, ...), custom_call_target="tpu_custom_call" | custom-call | tf_op jit(solution)/shard_map/partial/pallas_call | solution.py:326
  51.1 1.0 copy-done.3
  52.1 1.9 %add_convert_fusion.1 = bf16[768,768]{1,0:T(8,128)(2,1)S(1)} fusion(bf16[768,768]{1,0:T(8,128)(2,1)} %copy-done.3, bf16[768,768]{1,0:T(8,128)(2,1)} %get-tuple-element.31), kind=kLoop, calls=%fused_computation.1 | loop fusion | flops 2359296 | bytes 3538944 | tf_op jit(solution)/shard_map/convert_element_type | solution.py:368
  54.9 2.5 %collective-permute-start.4 = (bf16[384,768]{1,0:T(8,128)(2,1)}, bf16[384,768]{1,0:T(8,128)(2,1)}, u32[]{:S(2)}, u32[]{:S(2)}) collective-permute-start(bf16[384,768]{1,0:T(8,128)(2,1)} %dynamic-slice_bitcast_fusion.1), channel_id=1, source_target_pairs={{0,2},{1,3},{2,0},{3,1},{4,6},{5,7},{6,4},{7,5},{8,10},{9,11},{10,... | collective-permute-start | bytes 1769480 | tf_op jit(solution)/shard_map/ppermute | solution.py:29
  57.4 1.0 copy-done.1
  58.5 1.6 %add_convert_fusion = bf16[768,768]{1,0:T(8,128)(2,1)S(1)} fusion(bf16[768,768]{1,0:T(8,128)(2,1)S(1)} %copy-done.2, bf16[832,768]{1,0:T(8,128)(2,1)} %copy-done.1), kind=kLoop, calls=%fused_computation | loop fusion | flops 2359296 | bytes 3538944 | tf_op jit(solution)/shard_map/convert_element_type | solution.py:368
  60.1 0.9 add_convert_fusion.4
  61.0 0.9 pad_maximum_fusion.1
  61.9 4.0 %collective-permute-start.8 = (bf16[448,768]{1,0:T(8,128)(2,1)}, bf16[448,768]{1,0:T(8,128)(2,1)}, u32[]{:S(2)}, u32[]{:S(2)}) collective-permute-start(bf16[448,768]{1,0:T(8,128)(2,1)} %pad_maximum_fusion.1), channel_id=1, source_target_pairs={{0,4},{1,5},{2,6},{3,7},{4,0},{5,1},{6,2},{7,3},{8,12},{9,13},{10,... | collective-permute-start | bytes 2064392 | tf_op jit(solution)/shard_map/ppermute | solution.py:29
  65.9 5.8 %collective-permute-done.4 = bf16[384,768]{1,0:T(8,128)(2,1)} collective-permute-done((bf16[384,768]{1,0:T(8,128)(2,1)}, bf16[384,768]{1,0:T(8,128)(2,1)}, u32[]{:S(2)}, u32[]{:S(2)}) %collective-permute-start.4) | collective-permute-done | bytes 589856 | tf_op jit(solution)/shard_map/ppermute | solution.py:29
  71.7 1.2 fusion.1
  72.9 5.6 %collective-permute-start.5 = (bf16[192,768]{1,0:T(8,128)(2,1)S(1)}, bf16[192,768]{1,0:T(8,128)(2,1)}, u32[]{:S(2)}, u32[]{:S(2)}) collective-permute-start(bf16[192,768]{1,0:T(8,128)(2,1)S(1)} %dynamic-slice_bitcast_fusion.3), channel_id=1, source_target_pairs={{0,4},{1,5},{2,6},{3,7},{4,0},{5,1},{6,2},{7,3},{8,12},{9,13},{10,... | collective-permute-start | bytes 884744 | tf_op jit(solution)/shard_map/ppermute | solution.py:29
  78.5 4.0 %collective-permute-done.8 = bf16[448,768]{1,0:T(8,128)(2,1)} collective-permute-done((bf16[448,768]{1,0:T(8,128)(2,1)}, bf16[448,768]{1,0:T(8,128)(2,1)}, u32[]{:S(2)}, u32[]{:S(2)}) %collective-permute-start.8) | collective-permute-done | bytes 688160 | tf_op jit(solution)/shard_map/ppermute | solution.py:29
  82.5 1.2 fusion
  83.7 0.9 add_convert_fusion.3
  85.4 3.0 %collective-permute-start.9 = (bf16[256,768]{1,0:T(8,128)(2,1)}, bf16[256,768]{1,0:T(8,128)(2,1)S(1)}, u32[]{:S(2)}, u32[]{:S(2)}) collective-permute-start(bf16[256,768]{1,0:T(8,128)(2,1)} %pad_maximum_fusion.3), channel_id=1, source_target_pairs={{0,8},{1,9},{2,10},{3,11},{4,12},{5,13},{6,14},{7,15},{8,0},{9,1},... | collective-permute-start | bytes 1179656 | tf_op jit(solution)/shard_map/ppermute | solution.py:29
  88.5 17.2 %backward.1 = (bf16[512,1536]{1,0:T(8,128)(2,1)}, bf16[512,1536]{1,0:T(8,128)(2,1)}, bf16[512,1536]{1,0:T(8,128)(2,1)}, bf16[2,128,1536]{2,1,0:T(8,128)(2,1)}, f32[2,128,1536]{2,1,0:T(8,128)}) custom-call(bf16[512,1536]{1,0:T(8,128)(2,1)} %get-tuple-element.18.gh_ref.refs_2_, bf16[1536,1536]{1,0:T(8,128)(2,1)} %w_ref.1, bf16[512,1536]{1,0:T(8,128)(2,1)} %q_ref.3, ...), custom_call_target="tpu_custom_call" | custom-call | tf_op jit(solution)/shard_map/backward/pallas_call | solution.py:238
  105.7 1.3 %collective-permute-start.2 = (bf16[2,128,1536]{2,1,0:T(8,128)(2,1)}, bf16[2,128,1536]{2,1,0:T(8,128)(2,1)S(1)}, u32[]{:S(2)}, u32[]{:S(2)}) collective-permute-start(bf16[2,128,1536]{2,1,0:T(8,128)(2,1)} %get-tuple-element.27), channel_id=1, source_target_pairs={{1,0},{2,1},{3,2},{4,3},{5,4},{6,5},{7,6},{8,7},{9,8},{10,9},{11,1... | collective-permute-start | bytes 2359304 | tf_op jit(solution)/shard_map/ppermute | solution.py:24
  107.0 1.0 fusion.3
  108.1 2.9 %collective-permute-start.6 = (bf16[96,768]{1,0:T(8,128)(2,1)S(1)}, bf16[96,768]{1,0:T(8,128)(2,1)S(1)}, u32[]{:S(2)}, u32[]{:S(2)}) collective-permute-start(bf16[96,768]{1,0:T(8,128)(2,1)S(1)} %dynamic-slice_bitcast_fusion.5), channel_id=1, source_target_pairs={{0,8},{1,9},{2,10},{3,11},{4,12},{5,13},{6,14},{7,15},{8,0},{9,1},... | collective-permute-start | bytes 442376 | tf_op jit(solution)/shard_map/ppermute | solution.py:29
  112.1 2.5 %finish.1 = (bf16[512,1536]{1,0:T(8,128)(2,1)}, bf16[512,1536]{1,0:T(8,128)(2,1)}) custom-call(bf16[512,1536]{1,0:T(8,128)(2,1)} %get-tuple-element.24.gk_in, bf16[512,1536]{1,0:T(8,128)(2,1)} %get-tuple-element.25.gv_in, f32[2,128,1536]{2,1,0:T(8,128)} %get-tuple-element.26.last_ref, ...), custom_call_target="tpu_custom_call", output_to_operand_aliasing={{0}: (0, {}), {1}: (1, {})} | custom-call | tf_op jit(solution)/shard_map/finish/pallas_call | solution.py:273
  114.7 11.7 %collective-permute-done.6 = bf16[96,768]{1,0:T(8,128)(2,1)S(1)} collective-permute-done((bf16[96,768]{1,0:T(8,128)(2,1)S(1)}, bf16[96,768]{1,0:T(8,128)(2,1)S(1)}, u32[]{:S(2)}, u32[]{:S(2)}) %collective-permute-start.6) | collective-permute-done | bytes 147488 | tf_op jit(solution)/shard_map/ppermute | solution.py:29
  (42 shorter events, 5.3 us)
Async XLA Ops:
  0.6 5.9 %copy-start.7 = (s32[512]{0:T(512)S(1)}, s32[512]{0:T(512)}, u32[]{:S(2)}) copy-start(s32[512]{0:T(512)} %param.15) | copy-start | bytes 6148
  1.9 25.9 %collective-permute-start.1 = (bf16[2,128,1536]{2,1,0:T(8,128)(2,1)S(1)}, bf16[2,128,1536]{2,1,0:T(8,128)(2,1)S(1)}, u32[]{:S(2)}, u32[]{:S(2)}) collective-permute-start(bf16[2,128,1536]{2,1,0:T(8,128)(2,1)S(1)} %pad_maximum_fusion), channel_id=1, source_target_pairs={{0,1},{1,2},{2,3},{3,4},{4,5},{5,6},{6,7},{7,8},{8,9},{9,10},{10,1... | collective-permute-start | bytes 2359304 | tf_op jit(solution)/shard_map/ppermute | solution.py:24
  5.3 5.3 %collective-permute-start = (bf16[32,1536]{1,0:T(8,128)(2,1)S(1)}, bf16[32,1536]{1,0:T(8,128)(2,1)S(1)}, u32[]{:S(2)}, u32[]{:S(2)}) collective-permute-start(bf16[32,1536]{1,0:T(8,128)(2,1)S(1)} %slice.45), channel_id=1, source_target_pairs={{1,0},{2,1},{3,2},{4,3},{5,4},{6,5},{7,6},{8,7},{9,8},{10,9},{11,1... | collective-permute-start | bytes 294920 | tf_op jit(solution)/shard_map/ppermute | solution.py:24
  10.5 0.6 copy-start.6
  27.8 1.0 copy-start
  42.8 8.2 %collective-permute-start.3 = (bf16[768,768]{1,0:T(8,128)(2,1)}, bf16[768,768]{1,0:T(8,128)(2,1)S(1)}, u32[]{:S(2)}, u32[]{:S(2)}) collective-permute-start(bf16[768,768]{1,0:T(8,128)(2,1)} %get-tuple-element.32), channel_id=1, source_target_pairs={{0,1},{1,0},{2,3},{3,2},{4,5},{5,4},{6,7},{7,6},{8,9},{9,8},{10,11... | collective-permute-start | bytes 3538952 | tf_op jit(solution)/shard_map/ppermute | solution.py:29
  46.1 5.0 %copy-start.4 = (bf16[32,1536]{1,0:T(8,128)(2,1)S(1)}, bf16[32,1536]{1,0:T(8,128)(2,1)}, u32[]{:S(2)}) copy-start(bf16[32,1536]{1,0:T(8,128)(2,1)} %get-tuple-element.33.refs_3_.refs_4_) | copy-start | bytes 294916
  51.0 6.4 %collective-permute-start.7 = (bf16[832,768]{1,0:T(8,128)(2,1)}, bf16[832,768]{1,0:T(8,128)(2,1)S(1)}, u32[]{:S(2)}, u32[]{:S(2)}) collective-permute-start(bf16[832,768]{1,0:T(8,128)(2,1)} %get-tuple-element.35), channel_id=1, source_target_pairs={{0,1},{1,0},{2,3},{3,2},{4,5},{5,4},{6,7},{7,6},{8,9},{9,8},{10,11... | collective-permute-start | bytes 3833864 | tf_op jit(solution)/shard_map/ppermute | solution.py:29
  51.1 1.0 copy-start.3
  54.0 4.4 %copy-start.2 = (bf16[768,768]{1,0:T(8,128)(2,1)S(1)}, bf16[768,768]{1,0:T(8,128)(2,1)}, u32[]{:S(2)}) copy-start(bf16[768,768]{1,0:T(8,128)(2,1)} %get-tuple-element.34) | copy-start | bytes 3538948
  54.9 16.8 %collective-permute-start.4 = (bf16[384,768]{1,0:T(8,128)(2,1)}, bf16[384,768]{1,0:T(8,128)(2,1)}, u32[]{:S(2)}, u32[]{:S(2)}) collective-permute-start(bf16[384,768]{1,0:T(8,128)(2,1)} %dynamic-slice_bitcast_fusion.1), channel_id=1, source_target_pairs={{0,2},{1,3},{2,0},{3,1},{4,6},{5,7},{6,4},{7,5},{8,10},{9,11},{10,... | collective-permute-start | bytes 1769480 | tf_op jit(solution)/shard_map/ppermute | solution.py:29
  57.4 1.0 copy-start.1
  61.9 20.6 %collective-permute-start.8 = (bf16[448,768]{1,0:T(8,128)(2,1)}, bf16[448,768]{1,0:T(8,128)(2,1)}, u32[]{:S(2)}, u32[]{:S(2)}) collective-permute-start(bf16[448,768]{1,0:T(8,128)(2,1)} %pad_maximum_fusion.1), channel_id=1, source_target_pairs={{0,4},{1,5},{2,6},{3,7},{4,0},{5,1},{6,2},{7,3},{8,12},{9,13},{10,... | collective-permute-start | bytes 2064392 | tf_op jit(solution)/shard_map/ppermute | solution.py:29
  72.9 34.1 %collective-permute-start.5 = (bf16[192,768]{1,0:T(8,128)(2,1)S(1)}, bf16[192,768]{1,0:T(8,128)(2,1)}, u32[]{:S(2)}, u32[]{:S(2)}) collective-permute-start(bf16[192,768]{1,0:T(8,128)(2,1)S(1)} %dynamic-slice_bitcast_fusion.3), channel_id=1, source_target_pairs={{0,4},{1,5},{2,6},{3,7},{4,0},{5,1},{6,2},{7,3},{8,12},{9,13},{10,... | collective-permute-start | bytes 884744 | tf_op jit(solution)/shard_map/ppermute | solution.py:29
  85.4 25.5 %collective-permute-start.9 = (bf16[256,768]{1,0:T(8,128)(2,1)}, bf16[256,768]{1,0:T(8,128)(2,1)S(1)}, u32[]{:S(2)}, u32[]{:S(2)}) collective-permute-start(bf16[256,768]{1,0:T(8,128)(2,1)} %pad_maximum_fusion.3), channel_id=1, source_target_pairs={{0,8},{1,9},{2,10},{3,11},{4,12},{5,13},{6,14},{7,15},{8,0},{9,1},... | collective-permute-start | bytes 1179656 | tf_op jit(solution)/shard_map/ppermute | solution.py:29
  105.7 5.5 %collective-permute-start.2 = (bf16[2,128,1536]{2,1,0:T(8,128)(2,1)}, bf16[2,128,1536]{2,1,0:T(8,128)(2,1)S(1)}, u32[]{:S(2)}, u32[]{:S(2)}) collective-permute-start(bf16[2,128,1536]{2,1,0:T(8,128)(2,1)} %get-tuple-element.27), channel_id=1, source_target_pairs={{1,0},{2,1},{3,2},{4,3},{5,4},{6,5},{7,6},{8,7},{9,8},{10,9},{11,1... | collective-permute-start | bytes 2359304 | tf_op jit(solution)/shard_map/ppermute | solution.py:24
  108.1 18.3 %collective-permute-start.6 = (bf16[96,768]{1,0:T(8,128)(2,1)S(1)}, bf16[96,768]{1,0:T(8,128)(2,1)S(1)}, u32[]{:S(2)}, u32[]{:S(2)}) collective-permute-start(bf16[96,768]{1,0:T(8,128)(2,1)S(1)} %dynamic-slice_bitcast_fusion.5), channel_id=1, source_target_pairs={{0,8},{1,9},{2,10},{3,11},{4,12},{5,13},{6,14},{7,15},{8,0},{9,1},... | collective-permute-start | bytes 442376 | tf_op jit(solution)/shard_map/ppermute | solution.py:29
  111.1 15.3 %collective-permute-start.10 = (bf16[160,768]{1,0:T(8,128)(2,1)S(1)}, bf16[160,768]{1,0:T(8,128)(2,1)S(1)}, u32[]{:S(2)}, u32[]{:S(2)}) collective-permute-start(bf16[160,768]{1,0:T(8,128)(2,1)S(1)} %pad_maximum_fusion.4), channel_id=1, source_target_pairs={{0,2},{1,3},{2,0},{3,1},{4,6},{5,7},{6,4},{7,5},{8,10},{9,11},{10,... | collective-permute-start | bytes 737288 | tf_op jit(solution)/shard_map/ppermute | solution.py:29
  111.2 0.9 copy-start.5
